TPU v7x, 32 devices: a whole 2x2x4 slice. The times are simulated.
32 devices in a mesh: groups: 2 (over y), src: 8 (over z, x), tgt: 2 (over core).
Axes of the slice: x: 2, y: 2, z: 4, core: 2. Of those that a mesh axis runs over, the one named last changes fastest.
Arguments:
- source_points: bfloat16 [256, 64, 128], P(('groups', 'src')), parts along dimension 0, may hold values from -1.1 to 1.1
- target_points: bfloat16 [192, 64, 128], P(('groups', 'tgt')), parts along dimension 0, may hold values from -1.1 to 1.1
- source_logmass: float32 [32768], P(('groups', 'src')), parts along dimension 0, may hold values from -3 to 3
- target_logmass: float32 [24576], P(('groups', 'tgt')), parts along dimension 0, may hold values from -3 to 3
- warm_potential: float32 [24576], P(('groups', 'tgt')), parts along dimension 0, may hold values from -4 to 4
- block_ids: int32 [256, 2, 16], P(('groups', 'src'), 'tgt'), parts along dimension 0, may hold values from 0 to 47, as said below
- live_counts: int32 [256, 2], P(('groups', 'src'), 'tgt'), parts along dimension 0, may hold values from 1 to 16, as said below
Outputs:
- source_potential: float32 [32768], P(('groups', 'src')), parts along dimension 0
- target_potential: float32 [24576], P(('groups', 'tgt')), parts along dimension 0
There are 2 independent parts, one for each index of `groups`. A program takes and returns all parts, laid end to end along the dimension named above; each array names one. Nothing has to cross between parts.
Inputs may be any that keep to these rules, and one draw needn't show every extreme that they name: `block_ids`: the 16 ids of one source block and one target half are distinct; only the first live_counts slots belong to the support. A half may hold target blocks that no live slot names. `live_counts`: some source block has all 16 slots of its first half live.
All inputs are finite; a program needn't handle non-finite values.
Results may differ from a plain program's by a relative error of at most 0.0003.
Values sent between devices are 32-bit elements; how exact they have to be, the bound alone decides.
No kernel may reach another device: no remote copies, remote signals or barrier semaphores. Data moves between devices by JAX's collectives and lax.ppermute only.
A program may use at most 64 MiB of HBM per device.

v0:
```python
import jax
import jax.numpy as jnp
from jax import lax
from jax.sharding import PartitionSpec as P

ITERS = 2


epsilon = 0.1
lowest = -1e30
reach_limit = -1e29


def joined(part, axis, combine):
    gathered = jax.tree.map(lambda a: lax.all_gather(a, axis), part)

    def take(source):
        return jax.tree.map(lambda a: lax.dynamic_index_in_dim(a, source, 0, False), gathered)

    return lax.fori_loop(
        1, lax.axis_size(axis), lambda source, state: combine(state, take(source)), take(0)
    )


def pair_costs(source_sel, target_sel, source_sq, target_sq):
    products = jnp.einsum(
        "kdr,kdc->krc", source_sel, target_sel, preferred_element_type=jnp.float32
    )
    return source_sq[:, :, None] + target_sq[:, None, :] - 2.0 * products


def fold_into(best, total, member, tile_max, tile_sum):
    spread = jnp.where(member[:, :, None], tile_max[:, None, :], lowest)
    new_best = jnp.maximum(best, jnp.max(spread, axis=0))
    scaled = jnp.where(
        member[:, :, None],
        tile_sum[:, None, :] * jnp.exp(tile_max[:, None, :] - new_best[None]),
        0.0,
    )
    return (new_best, total * jnp.exp(best - new_best) + jnp.sum(scaled, axis=0))


def combine_pairs(first, second):
    highest = jnp.maximum(first[0], second[0])
    return (
        highest,
        first[1] * jnp.exp(first[0] - highest) + second[1] * jnp.exp(second[0] - highest),
    )


def per_device(
    source_points,
    target_points,
    source_logmass,
    target_logmass,
    warm_potential,
    block_ids,
    live_counts,
):
    row_blocks = source_points.shape[0]
    block_size = source_points.shape[2]
    target_blocks = target_points.shape[0]
    slot_count = block_ids.shape[2]
    source_sq = jnp.sum(jnp.square(source_points.astype(jnp.float32)), axis=1)
    target_sq = jnp.sum(jnp.square(target_points.astype(jnp.float32)), axis=1)
    slot_ids = block_ids[:, 0, :]
    slot_live = jnp.arange(slot_count, dtype=jnp.int32)[None, :] < live_counts[:, 0][:, None]
    source_mass = source_logmass.reshape(row_blocks, block_size)
    target_mass = target_logmass.reshape(target_blocks, block_size)
    potential = warm_potential.reshape(target_blocks, block_size)
    row_range = jnp.arange(row_blocks, dtype=jnp.int32)
    block_range = jnp.arange(target_blocks, dtype=jnp.int32)
    owner_rows = jnp.broadcast_to(row_range[:, None], (row_blocks, slot_count))

    def sweep(group_fn, initial):

        def advance(state, group):
            return (group_fn(state, group[0], group[1], group[2]), None)

        return lax.scan(advance, initial, (owner_rows, slot_ids, slot_live))[0]

    def group_costs(rows_sel, ids_sel):
        return pair_costs(
            source_points[rows_sel], target_points[ids_sel], source_sq[rows_sel], target_sq[ids_sel]
        )

    source_potential = jnp.zeros((row_blocks, block_size), jnp.float32)
    for sweep_index in range(ITERS):

        def row_group(state, rows_sel, ids_sel, live_sel):
            scores = (potential[ids_sel][:, None, :] - group_costs(rows_sel, ids_sel)) / epsilon
            tile_max = jnp.max(scores, axis=2)
            tile_sum = jnp.sum(jnp.exp(scores - tile_max[:, :, None]), axis=2)
            tile_max = jnp.where(live_sel[:, None], tile_max, lowest)
            tile_sum = jnp.where(live_sel[:, None], tile_sum, 0.0)
            member = (rows_sel[:, None] == row_range[None, :]) & live_sel[:, None]
            return fold_into(state[0], state[1], member, tile_max, tile_sum)

        row_start = (
            jnp.full((row_blocks, block_size), lowest, jnp.float32),
            jnp.zeros((row_blocks, block_size), jnp.float32),
        )
        row_best, row_total = sweep(row_group, row_start)
        row_best, row_total = joined((row_best, row_total), "tgt", combine_pairs)
        source_potential = epsilon * source_mass - epsilon * (row_best + jnp.log(row_total))

        def column_group(state, rows_sel, ids_sel, live_sel):
            scores = (
                source_potential[rows_sel][:, :, None] - group_costs(rows_sel, ids_sel)
            ) / epsilon
            tile_max = jnp.max(scores, axis=1)
            tile_sum = jnp.sum(jnp.exp(scores - tile_max[:, None, :]), axis=1)
            tile_max = jnp.where(live_sel[:, None], tile_max, lowest)
            tile_sum = jnp.where(live_sel[:, None], tile_sum, 0.0)
            member = (ids_sel[:, None] == block_range[None, :]) & live_sel[:, None]
            return fold_into(state[0], state[1], member, tile_max, tile_sum)

        column_start = (
            jnp.full((target_blocks, block_size), lowest, jnp.float32),
            jnp.zeros((target_blocks, block_size), jnp.float32),
        )
        column_best, column_total = sweep(column_group, column_start)
        merged_best, merged_total = joined((column_best, column_total), "src", combine_pairs)
        reached = merged_best > reach_limit
        log_total = jnp.where(
            reached, merged_best + jnp.log(jnp.where(reached, merged_total, 1.0)), 0.0
        )
        potential = epsilon * target_mass - epsilon * log_total
    return (source_potential.reshape(-1), potential.reshape(-1))


def solution(mesh):
    in_specs = (
        P(("groups", "src"), None, None),
        P(("groups", "tgt"), None, None),
        P(("groups", "src")),
        P(("groups", "tgt")),
        P(("groups", "tgt")),
        P(("groups", "src"), "tgt", None),
        P(("groups", "src"), "tgt"),
    )
    out_specs = (P(("groups", "src")), P(("groups", "tgt")))
    return jax.shard_map(
        per_device, mesh=mesh, in_specs=in_specs, out_specs=out_specs, check_vma=False
    )
```

profile of v0, /device:TPU:0, one launch (start us, length us, event | category | flops | bytes accessed | tf_op | source)
XLA Modules:
  0.0 511.9 jit_solution(15847013125974729550)
XLA Ops:
  0.7 1.4 multiply_reduce_fusion
  3.3 87.1 %while.100 = (s32[]{:T(128)}, f32[16,128]{1,0:T(8,128)S(1)}, f32[16,128]{1,0:T(8,128)S(1)}, s32[16,16]{1,0:T(8,128)S(1)}, pred[16,16]{1,0:T(8,128)(4,1)S(1)}, /*...) while((s32[]{:T(128)}, f32[16,128]{1,0:T(8,128)S(1)}, ...), condition=%wide.region_7.8_spmd.clone, body=%wide.region_2.7_spmd.clone.sunk | while | flops 35861088 | bytes 3942228 | solution.py:80
  6.9 1.2 fusion.112
  12.3 1.2 fusion.112
  17.8 1.2 fusion.112
  23.2 1.2 fusion.112
  28.7 1.2 fusion.112
  34.1 1.2 fusion.112
  39.6 1.2 fusion.112
  45.0 1.2 fusion.112
  50.4 1.2 fusion.112
  55.9 1.2 fusion.112
  61.3 1.2 fusion.112
  66.8 1.2 fusion.112
  72.2 1.2 fusion.112
  90.4 1.9 all-gather
  92.3 1.8 all-gather.1
  94.2 100.3 %while.101 = (s32[]{:T(128)}, f32[48,128]{1,0:T(8,128)S(1)}, f32[48,128]{1,0:T(8,128)S(1)}, s32[16,16]{1,0:T(8,128)}, pred[16,16]{1,0:T(8,128)(4,1)S(1)}, /*inde...) while((s32[]{:T(128)}, f32[48,128]{1,0:T(8,128)S(1)}, ...), condition=%wide.region_13.14_spmd.clone, body=%wide.region_8.13_spmd.clone.sunk | while | flops 36275808 | bytes 4156756 | solution.py:80
  122.9 1.2 fusion.119
  154.2 1.2 fusion.119
  185.6 1.2 fusion.119
  194.5 32.3 %all-gather.2 = f32[384,128]{1,0:T(8,128)S(1)} all-gather(f32[48,128]{1,0:T(8,128)S(1)} %get-tuple-element.558), channel_id=4, replica_groups=mesh['groups'=2,'src'=8,'tgt'=2] {'src'}, dimensions={0}, use_global_device_ids=true | all-gather | bytes 221184 | tf_op jit(solution)/shard_map/all_gather | solution.py:15
  226.8 30.6 %all-gather.3 = f32[384,128]{1,0:T(8,128)S(1)} all-gather(f32[48,128]{1,0:T(8,128)S(1)} %get-tuple-element.559), channel_id=5, replica_groups=mesh['groups'=2,'src'=8,'tgt'=2] {'src'}, dimensions={0}, use_global_device_ids=true | all-gather | bytes 221184 | tf_op jit(solution)/shard_map/all_gather | solution.py:15
  257.9 87.1 %while.102 = (s32[]{:T(128)}, f32[16,128]{1,0:T(8,128)S(1)}, f32[16,128]{1,0:T(8,128)S(1)}, s32[16,16]{1,0:T(8,128)S(1)}, pred[16,16]{1,0:T(8,128)(4,1)S(1)}, /*...) while((s32[]{:T(128)}, f32[16,128]{1,0:T(8,128)S(1)}, ...), condition=%wide.region_21.22_spmd.clone, body=%wide.region_16.21_spmd.clone.sunk | while | flops 35861088 | bytes 3942228 | solution.py:80
  345.0 1.8 all-gather.4
  346.8 1.8 all-gather.5
  348.7 100.3 %while.103 = (s32[]{:T(128)}, f32[48,128]{1,0:T(8,128)S(1)}, f32[48,128]{1,0:T(8,128)S(1)}, s32[16,16]{1,0:T(8,128)}, pred[16,16]{1,0:T(8,128)(4,1)S(1)}, /*inde...) while((s32[]{:T(128)}, f32[48,128]{1,0:T(8,128)S(1)}, ...), condition=%wide.region_27.28_spmd.clone, body=%wide.region_22.27_spmd.clone.sunk | while | flops 36275808 | bytes 4156756 | solution.py:80
  371.1 1.2 fusion.133
  402.5 1.2 fusion.133
  433.8 1.2 fusion.133
  449.0 30.6 %all-gather.6 = f32[384,128]{1,0:T(8,128)S(1)} all-gather(f32[48,128]{1,0:T(8,128)S(1)} %get-tuple-element.564), channel_id=8, replica_groups=mesh['groups'=2,'src'=8,'tgt'=2] {'src'}, dimensions={0}, use_global_device_ids=true | all-gather | bytes 221184 | tf_op jit(solution)/shard_map/all_gather | solution.py:15
  479.7 30.6 %all-gather.7 = f32[384,128]{1,0:T(8,128)S(1)} all-gather(f32[48,128]{1,0:T(8,128)S(1)} %get-tuple-element.565), channel_id=9, replica_groups=mesh['groups'=2,'src'=8,'tgt'=2] {'src'}, dimensions={0}, use_global_device_ids=true | all-gather | bytes 221184 | tf_op jit(solution)/shard_map/all_gather | solution.py:15
  (1248 shorter events, 349.1 us)
Async XLA Ops:
  0.6 2.6 copy-start.1
  0.6 2.6 copy-start
  0.7 2.5 copy-start.5
  0.7 2.6 copy-start.2
  3.2 90.9 %copy-start.4 = (f32[2048]{0:T(1024)S(1)}, f32[2048]{0:T(1024)}, u32[]{:S(2)}) copy-start(f32[2048]{0:T(1024)} %param.21) | copy-start | bytes 24580
  194.5 63.3 %copy-start.3 = (f32[6144]{0:T(1024)S(1)}, f32[6144]{0:T(1024)}, u32[]{:S(2)}) copy-start(f32[6144]{0:T(1024)} %param.22) | copy-start | bytes 73732
where the time goes:
time: 516 us; the launch traced here: 512 us
  local copies, waits for them, and re-layouts  208 us (40%)
  blocking collectives  132 us (26%)
  other arithmetic  88.8 us (17%)
  matrix products  75.5 us (15%)
  loops' own time  7.22 us (1%)
    all_gather x8, blocking collectives, joined(): gathered = jax.tree.map(lambda a: lax.all_gather(a, axis), part)  132 us
    dot_general x64, matrix products, pair_costs(): jnp.einsum('kdr,kdc->krc', source_sel, target_sel, preferred_element_type...  75.5 us
    gather x64, local copies, waits for them, and re-layouts, group_costs(): source_points[rows_sel]  38.2 us
    gather x64, local copies, waits for them, and re-layouts, group_costs(): target_points[ids_sel]  38.2 us
    gather x64, local copies, waits for them, and re-layouts, group_costs(): target_sq[ids_sel]  36 us
    gather x64, local copies, waits for them, and re-layouts, group_costs(): source_sq[rows_sel]  36 us
    select_n x32, other arithmetic, group_costs(): source_sq[rows_sel]  22.3 us
    select_n x32, other arithmetic, group_costs(): target_sq[ids_sel]  22.3 us

commit v1 on v0

v1 whole, which is shorter than its diff:
```python
import functools
import math

import jax
import jax.numpy as jnp
from jax import lax
from jax.experimental import pallas as pl
from jax.experimental.pallas import tpu as pltpu
from jax.sharding import PartitionSpec as P

ITERS = 2
epsilon = 0.1
lowest = -1.0e30
reach_limit = -1.0e29

LOG2E = math.log2(math.e)
SCALE = LOG2E / epsilon
UNSCALE = epsilon / LOG2E
SHIFT = 60.0
SUM_LOW = 2.0**-30
SUM_HIGH = 2.0**126
WEIGHT_LOW = 2.0**-125
GROUP = 4


def log_add(first, second):
    highest = jnp.maximum(first, second)
    return highest + jnp.log2(jnp.exp2(first - highest) + jnp.exp2(second - highest))


def log_sum(parts):
    highest = functools.reduce(jnp.maximum, parts)
    total = functools.reduce(jnp.add, [jnp.exp2(part - highest) for part in parts])
    return highest + jnp.log2(total)


def out_of_range(sums, mask=None):
    good = (sums >= SUM_LOW) & (sums <= SUM_HIGH)
    if mask is not None:
        good = good | jnp.logical_not(mask)
    return jnp.max(jnp.where(good, 0.0, 1.0)) > 0.5


def make_kernels(rows, targets, slots, feat, blk):
    per_row = slots // GROUP
    groups = rows * per_row
    padded = targets + 8

    def slot(ids, counts, code, u):
        row = code // per_row
        row_at = jnp.minimum(row, rows - 1)
        k = (code % per_row) * GROUP + u
        target = ids[row_at, k]
        live = (row < rows) & (k < counts[row_at, 0])
        return row, row_at, target, jnp.where(live, target, targets)

    def tile_scores(x, y, row, target):
        return lax.dot_general(
            x[row], y[target], (((0,), (0,)), ((), ())), preferred_element_type=jnp.float32
        ) * (2.0 * SCALE)

    def slow_rows(ids, counts, x_hbm, y_hbm, weight_log, out):
        def run(x, y):
            pltpu.sync_copy(x_hbm, x)
            pltpu.sync_copy(y_hbm, y)

            @pl.loop(0, rows)
            def _(row):
                def body(k, state):
                    target = ids[row, k]
                    score = tile_scores(x, y, row, target) + weight_log[pl.ds(target, 1), :]
                    score = score.T
                    best = jnp.maximum(state[0], jnp.max(score, axis=0, keepdims=True))
                    total = state[1] * jnp.exp2(state[0] - best)
                    total += jnp.sum(jnp.exp2(score - best), axis=0, keepdims=True)
                    return best, total

                start = (jnp.full((1, blk), lowest, jnp.float32), jnp.zeros((1, blk), jnp.float32))
                best, total = lax.fori_loop(0, counts[row, 0], body, start)
                out[pl.ds(row, 1), :] = best + jnp.log2(total)

        pl.run_scoped(
            run,
            pltpu.VMEM((rows, feat, blk), jnp.bfloat16),
            pltpu.VMEM((targets, feat, blk), jnp.bfloat16),
        )

    def slow_columns(ids, counts, x_hbm, y_hbm, weight_log, out):
        def run(x, y, total):
            pltpu.sync_copy(x_hbm, x)
            pltpu.sync_copy(y_hbm, y)
            out[...] = jnp.full((targets, blk), lowest, jnp.float32)
            total[...] = jnp.zeros((targets, blk), jnp.float32)

            @pl.loop(0, rows)
            def _(row):
                @pl.loop(0, counts[row, 0])
                def _(k):
                    target = ids[row, k]
                    score = (tile_scores(x, y, row, target).T + weight_log[pl.ds(row, 1), :]).T
                    old = out[pl.ds(target, 1), :]
                    best = jnp.maximum(old, jnp.max(score, axis=0, keepdims=True))
                    add = jnp.sum(jnp.exp2(score - best), axis=0, keepdims=True)
                    total[pl.ds(target, 1), :] = (
                        total[pl.ds(target, 1), :] * jnp.exp2(old - best) + add
                    )
                    out[pl.ds(target, 1), :] = best

            best = out[...]
            reached = best > reach_limit
            out[...] = jnp.where(
                reached, best + jnp.log2(jnp.where(reached, total[...], 1.0)), lowest
            )

        pl.run_scoped(
            run,
            pltpu.VMEM((rows, feat, blk), jnp.bfloat16),
            pltpu.VMEM((targets, feat, blk), jnp.bfloat16),
            pltpu.VMEM((targets, blk), jnp.float32),
        )

    def list_groups(counts, work):
        def add(row, n):
            for g in range(per_row):
                work[n + g] = row * per_row + g
            return n + (counts[row, 0] + GROUP - 1) // GROUP

        n = lax.fori_loop(0, rows, add, 0)
        for g in range(4):
            work[n + g] = groups
        return n

    def row_weights(log_weight, weights):
        top = jnp.max(log_weight)
        values = jnp.exp2(log_weight - (top - SHIFT))
        weights[0:targets, :] = values
        weights[targets:padded, :] = jnp.zeros((padded - targets, blk), jnp.float32)
        return top, jnp.min(values) < WEIGHT_LOW

    def finish_rows(acc, top, flushed, log_weight, ids, counts, x_hbm, y_hbm, out, sums):
        for row in range(rows):
            sums[row : row + 1, :] = jnp.sum(acc[row].T, axis=0, keepdims=True)
        found = sums[...]
        out[...] = jnp.log2(found) + (top - SHIFT)

        @pl.when(flushed | out_of_range(found))
        def _():
            slow_rows(ids, counts, x_hbm, y_hbm, log_weight, out)

    def first_rows(
        ids, counts, x, y, x_hbm, y_hbm, warm,
        out, tiles, target_sq, member, work, n_work,
        acc, weights, log_weight, x_rows, even, odd, sums,
    ):
        n = list_groups(counts, work)
        n_work[0] = n
        for target in range(targets):
            values = y[target].astype(jnp.float32)
            target_sq[target : target + 1, :] = jnp.sum(values * values, axis=0, keepdims=True)
        log_weight[...] = (warm[...] - target_sq[...]) * SCALE
        top, flushed = row_weights(log_weight[...], weights)
        member[...] = jnp.zeros(member.shape, jnp.float32)
        for row in range(rows):
            x_rows[row] = x[row].T
        acc[...] = jnp.zeros(acc.shape, jnp.float32)

        def products(code, buffer):
            for u in range(GROUP):
                _, row_at, target, _ = slot(ids, counts, code, u)
                buffer[u] = jnp.dot(x_rows[row_at], y[target], preferred_element_type=jnp.float32)

        def consume(code, buffer):
            row = code // per_row
            total = acc[row]
            for u in range(GROUP):
                _, _, _, weight_at = slot(ids, counts, code, u)
                value = jnp.exp2(buffer[u] * (2.0 * SCALE))
                tiles[code * GROUP + u] = value
                total += value * weights[pl.ds(weight_at, 1), :]
                member[pl.ds(weight_at, 1), :] = jnp.ones((1, blk), jnp.float32)
            acc[row] = total

        products(work[0], even)

        @pl.loop(0, (n + 1) // 2)
        def _(pair):
            products(work[2 * pair + 1], odd)
            consume(work[2 * pair], even)
            products(work[2 * pair + 2], even)
            consume(work[2 * pair + 1], odd)

        finish_rows(acc, top, flushed, log_weight, ids, counts, x_hbm, y_hbm, out, sums)

    def later_rows(
        ids, counts, work, n_work, tiles, x_hbm, y_hbm, parts, target_mass, target_sq,
        out,
        acc, weights, log_weight, sums,
    ):
        merged = parts[...]
        reached = merged > reach_limit
        log_weight[...] = target_mass[...] * LOG2E - jnp.where(
            reached, merged, target_sq[...] * SCALE
        )
        top, flushed = row_weights(log_weight[...], weights)
        acc[...] = jnp.zeros(acc.shape, jnp.float32)

        def consume(code):
            row = code // per_row
            total = acc[row]
            for u in range(GROUP):
                _, _, _, weight_at = slot(ids, counts, code, u)
                total += tiles[code * GROUP + u] * weights[pl.ds(weight_at, 1), :]
            acc[row] = total

        @pl.loop(0, (n_work[0] + 1) // 2)
        def _(pair):
            consume(work[2 * pair])
            consume(work[2 * pair + 1])

        finish_rows(acc, top, flushed, log_weight, ids, counts, x_hbm, y_hbm, out, sums)

    def columns(
        last, ids, counts, work, n_work, tiles, x_hbm, y_hbm, own, other, source_mass, member,
        *rest,
    ):
        if last:
            x, out, potential, acc, weights, sums, log_weight = rest
        else:
            out, acc, weights, sums, log_weight = rest
        log_weight[...] = source_mass[...] * LOG2E - log_add(own[...], other[...])
        if last:
            for row in range(rows):
                values = x[row].astype(jnp.float32)
                source_sq = jnp.sum(values * values, axis=0, keepdims=True)
                potential[row : row + 1, :] = log_weight[row : row + 1, :] * UNSCALE + source_sq
        top = jnp.max(log_weight[...])
        values = jnp.exp2(log_weight[...] - (top - SHIFT))
        flushed = jnp.min(values) < WEIGHT_LOW
        for row in range(rows):
            weights[row] = jnp.broadcast_to(values[row : row + 1, :], (blk, blk)).T
        acc[...] = jnp.zeros(acc.shape, jnp.float32)

        def consume(code):
            row_at = jnp.minimum(code // per_row, rows - 1)
            weight = weights[row_at]
            for u in range(GROUP):
                _, _, _, target = slot(ids, counts, code, u)
                value = (tiles[code * GROUP + u] * weight).reshape(blk // 8, 8, blk)
                acc[target] += jnp.sum(value, axis=0)

        @pl.loop(0, (n_work[0] + 1) // 2)
        def _(pair):
            consume(work[2 * pair])
            consume(work[2 * pair + 1])

        for target in range(targets):
            sums[target : target + 1, :] = jnp.sum(acc[target], axis=0, keepdims=True)
        found = sums[...]
        reached = member[0:targets, :] > 0.5
        out[...] = jnp.where(
            reached, jnp.log2(jnp.where(reached, found, 1.0)) + (top - SHIFT), lowest
        )

        @pl.when(flushed | out_of_range(found, reached))
        def _():
            slow_columns(ids, counts, x_hbm, y_hbm, log_weight, out)

    smem = pl.BlockSpec(memory_space=pltpu.SMEM)
    vmem = pl.BlockSpec(memory_space=pltpu.VMEM)
    anywhere = pl.BlockSpec(memory_space=pl.ANY)
    f32 = jnp.float32
    limit = pltpu.CompilerParams(vmem_limit_bytes=20 * 1024 * 1024)

    first_rows_call = pl.pallas_call(
        first_rows,
        name="first_rows",
        in_specs=[smem, smem, vmem, vmem, anywhere, anywhere, vmem],
        out_specs=[vmem, vmem, vmem, vmem, smem, smem],
        out_shape=[
            jax.ShapeDtypeStruct((rows, blk), f32),
            pltpu.VMEM(((groups + 1) * GROUP, blk, blk), f32),
            jax.ShapeDtypeStruct((targets, blk), f32),
            jax.ShapeDtypeStruct((padded, blk), f32),
            jax.ShapeDtypeStruct((groups + 8,), jnp.int32),
            jax.ShapeDtypeStruct((1,), jnp.int32),
        ],
        scratch_shapes=[
            pltpu.VMEM((rows + 1, blk, blk), f32),
            pltpu.VMEM((padded, blk), f32),
            pltpu.VMEM((targets, blk), f32),
            pltpu.VMEM((rows, blk, feat), jnp.bfloat16),
            pltpu.VMEM((GROUP, blk, blk), f32),
            pltpu.VMEM((GROUP, blk, blk), f32),
            pltpu.VMEM((rows, blk), f32),
        ],
        compiler_params=limit,
    )
    later_rows_call = pl.pallas_call(
        later_rows,
        name="later_rows",
        in_specs=[smem, smem, smem, smem, vmem, anywhere, anywhere, vmem, vmem, vmem],
        out_specs=vmem,
        out_shape=jax.ShapeDtypeStruct((rows, blk), f32),
        scratch_shapes=[
            pltpu.VMEM((rows + 1, blk, blk), f32),
            pltpu.VMEM((padded, blk), f32),
            pltpu.VMEM((targets, blk), f32),
            pltpu.VMEM((rows, blk), f32),
        ],
        compiler_params=limit,
    )

    def columns_call(last):
        outs = [jax.ShapeDtypeStruct((targets, blk), f32)]
        if last:
            outs.append(jax.ShapeDtypeStruct((rows, blk), f32))
        return pl.pallas_call(
            functools.partial(columns, last),
            name="last_columns" if last else "columns",
            in_specs=[smem] * 4 + [vmem, anywhere, anywhere] + [vmem] * (5 if last else 4),
            out_specs=[vmem] * len(outs),
            out_shape=outs,
            scratch_shapes=[
                pltpu.VMEM((padded, 8, blk), f32),
                pltpu.VMEM((rows, blk, blk), f32),
                pltpu.VMEM((targets, blk), f32),
                pltpu.VMEM((rows, blk), f32),
            ],
            compiler_params=limit,
        )

    return first_rows_call, later_rows_call, columns_call


def joined_over_sources(part):
    size = lax.axis_size("src")
    step = 1
    while step < size:
        width = 4 if step == 1 and size % 4 == 0 else 2
        parts = [part] + [
            lax.ppermute(part, "src", [(i, i ^ (step * k)) for i in range(size)])
            for k in range(1, width)
        ]
        part = log_sum(parts)
        step *= width
    return part


def per_device(
    source_points,
    target_points,
    source_logmass,
    target_logmass,
    warm_potential,
    block_ids,
    live_counts,
):
    rows, feat, blk = source_points.shape
    targets = target_points.shape[0]
    slots = block_ids.shape[2]
    ids = block_ids.reshape(rows, slots)
    source_mass = source_logmass.reshape(rows, blk)
    target_mass = target_logmass.reshape(targets, blk)
    warm = warm_potential.reshape(targets, blk)
    first_rows, later_rows, columns = make_kernels(rows, targets, slots, feat, blk)
    swap = [(i, i ^ 1) for i in range(lax.axis_size("tgt"))]

    part, tiles, target_sq, member, work, n_work = first_rows(
        ids, live_counts, source_points, target_points, source_points, target_points, warm
    )
    tiles = pltpu.with_memory_space_constraint(tiles, pltpu.VMEM)
    for sweep_index in range(ITERS):
        last = sweep_index == ITERS - 1
        common = (ids, live_counts, work, n_work, tiles, source_points, target_points)
        if sweep_index > 0:
            part = later_rows(*common, merged, target_mass, target_sq)
        other = lax.ppermute(part, "tgt", swap)
        found = columns(last)(
            *common, part, other, source_mass, member, *([source_points] if last else [])
        )
        merged = joined_over_sources(found[0])
    source_potential = found[1]
    log_total = jnp.where(
        merged > reach_limit, merged * UNSCALE - target_sq, 0.0
    )
    potential = epsilon * target_mass - log_total
    return (source_potential.reshape(-1), potential.reshape(-1))


def solution(mesh):
    in_specs = (
        P(("groups", "src"), None, None),
        P(("groups", "tgt"), None, None),
        P(("groups", "src")),
        P(("groups", "tgt")),
        P(("groups", "tgt")),
        P(("groups", "src"), "tgt", None),
        P(("groups", "src"), "tgt"),
    )
    out_specs = (P(("groups", "src")), P(("groups", "tgt")))
    return jax.shard_map(
        per_device, mesh=mesh, in_specs=in_specs, out_specs=out_specs, check_vma=False
    )
```

time: 516 us -> 338 us (0.66); the launches traced: 512 us -> 341 us
  Pallas kernels: 0 us -> 275 us
  local copies, waits for them, and re-layouts: 208 us -> 4.95 us
  blocking collectives: 132 us -> 0 us
  other arithmetic: 88.8 us -> 0.75 us
  matrix products: 75.5 us -> 0 us
  starting transfers between devices: 0 us -> 46.9 us
  waiting for transfers between devices: 0 us -> 12.9 us
  loops' own time: 7.22 us -> 0 us
    pallas_call x0 -> x4, Pallas kernels: none -> 275 us  [the longest x2 148 us: per_device(): columns(last)]
    gather x320 -> x0, local copies, waits for them, and re-layouts: 184 us -> none  [the longest x64 38.2 us: group_costs(): source_points[rows_sel]]
    all_gather x8 -> x0, blocking collectives: 132 us -> none  [joined(): gathered = jax.tree.map(lambda a: lax.all_gather(a, axis), part)]
    dot_general x64 -> x0, matrix products: 75.5 us -> none  [pair_costs(): jnp.einsum('kdr,kdc->krc', source_sel, target_sel, preferred_element_type...]
    select_n x128 -> x0, other arithmetic: 49.4 us -> none  [the longest x32 22.3 us: group_costs(): source_sq[rows_sel]]
    ppermute x0 -> x10, starting transfers between devices: none -> 46.9 us  [the longest x8 39.3 us: joined_over_sources(): lax.ppermute(part, 'src', [(i, i ^ step * k) for i in range(size)])]
    eq x64 -> x0, local copies, waits for them, and re-layouts: 22.4 us -> none  [the longest x32 22.2 us: column_group(): member = (ids_sel[:, None] == block_range[None, :]) & live_sel[:, None]]
    reduce_sum x130 -> x0, other arithmetic: 21.5 us -> none  [the longest x64 8.66 us: fold_into(): jnp.sum(scaled, axis=0)]
  transfers between devices with their start and end apart: 0 -> 10, of which waited for: 0 -> 8; matrix products, arithmetic and copies ran while one was open for 0% -> 0% of each run, Pallas kernels for 0% -> 0%
where the time goes in v1:
time: 338 us; the launch traced here: 341 us
  Pallas kernels  275 us (81%)
  starting transfers between devices  46.9 us (14%)
  waiting for transfers between devices  12.9 us (4%)
  local copies, waits for them, and re-layouts  4.95 us (1%)
    pallas_call x2, Pallas kernels, per_device(): columns(last)  148 us
    pallas_call x1, Pallas kernels, per_device(): first_rows(ids, live_counts, source_points, target_points, source_points,...  65.9 us
    pallas_call x1, Pallas kernels, per_device(): part = later_rows(*common, merged, target_mass, target_sq)  61.2 us
    ppermute x8, starting transfers between devices, joined_over_sources(): lax.ppermute(part, 'src', [(i, i ^ step * k) for i in range(size)])  39.3 us
    ppermute x8, waiting for transfers between devices, joined_over_sources(): lax.ppermute(part, 'src', [(i, i ^ step * k) for i in range(size)])  11.2 us
    ppermute x2, starting transfers between devices, per_device(): other = lax.ppermute(part, 'tgt', swap)  7.59 us
  transfers between devices with their start and end apart: 10, of which 8 were waited for; matrix products, arithmetic and copies ran while one was open for 0% of the time, Pallas kernels for 0%

profile of v1, /device:TPU:0, one launch (start us, length us, event | category | flops | bytes accessed | tf_op | source)
XLA Modules:
  0.0 341.4 jit_solution(6246195195602781711)
XLA Ops:
  0.6 0.7 copy.12.counts
  1.4 1.1 copy-done
  2.5 0.9 copy-done.1
  3.4 0.7 copy-done.2
  4.1 0.7 copy-done.5
  4.9 65.9 %first_rows.1 = (f32[16,128]{1,0:T(8,128)S(1)}, f32[260,128,128]{2,1,0:T(8,128)S(1)}, f32[48,128]{1,0:T(8,128)S(1)}, f32[56,128]{1,0:T(8,128)S(1)}, s32[72]{0:T(128)S(1)}, /*index=5*/s32[1]{0:T(128)}) custom-call(s32[16,16]{1,0:T(8,128)S(1)} %bitcast.8, s32[16,1]{1,0:T(8,128)S(1)} %copy.12.counts, bf16[16,64,128]{2,1,0:T(8,128)(2,1)S(1)} %copy-done.1, ...), custom_call_target="tpu_custom_call" | custom-call | tf_op jit(solution)/shard_map/first_rows/pallas_call | solution.py:368
  70.8 7.2 %collective-permute-start = (f32[16,128]{1,0:T(8,128)S(1)}, f32[16,128]{1,0:T(8,128)S(1)}, u32[]{:S(2)}, u32[]{:S(2)}) collective-permute-start(f32[16,128]{1,0:T(8,128)S(1)} %get-tuple-element.13.own), channel_id=1, source_target_pairs={{0,1},{1,0},{2,3},{3,2},{4,5},{5,4},{6,7},{7,6},{8,9},{9,8},{10,11... | collective-permute-start | bytes 24584 | tf_op jit(solution)/shard_map/ppermute | solution.py:377
  78.1 0.8 collective-permute-done.other
  78.9 0.7 copy-done.4
  79.6 73.7 %columns.1 = f32[48,128]{1,0:T(8,128)S(1)} custom-call(s32[16,16]{1,0:T(8,128)S(1)} %bitcast.9, s32[16,1]{1,0:T(8,128)S(1)} %copy.12.counts, s32[72]{0:T(128)S(1)} %get-tuple-element.10.work, s32[1]{0:T(128)} %get-tuple-element.11.n_work, f32[260,128,128]{2,1,0:T(8,128)S(1)} %get-tuple-element.12.tiles, bf16[16,64,128]{2,1,0:T(8,128)(2,1)S(1)} %copy-done.1, ...), custom_call_target="tpu_custom_call" | custom-call | tf_op jit(solution)/shard_map/columns/pallas_call | solution.py:378
  153.3 0.1 collective-permute-start.3
  153.4 14.2 %collective-permute-start.2 = (f32[48,128]{1,0:T(8,128)S(1)}, f32[48,128]{1,0:T(8,128)S(1)}, u32[]{:S(2)}, u32[]{:S(2)}) collective-permute-start(f32[48,128]{1,0:T(8,128)S(1)} %columns.1), channel_id=1, source_target_pairs={{0,4},{2,6},{4,0},{6,2},{8,12},{10,14},{12,8},{14,10},{1,5},{3,7},... | collective-permute-start | bytes 73736 | tf_op jit(solution)/shard_map/ppermute | solution.py:341
  167.6 1.4 collective-permute-start.1
  168.9 0.0 collective-permute-done.3
  168.9 0.6 collective-permute-done.2
  169.5 1.8 collective-permute-done.1
  171.4 2.1 collective-permute-start.4
  173.5 2.7 collective-permute-done.4
  176.2 0.0 copy-done.3
  176.2 61.2 %later_rows.1.own = f32[16,128]{1,0:T(8,128)S(1)} custom-call(s32[16,16]{1,0:T(8,128)S(1)} %bitcast.10, s32[16,1]{1,0:T(8,128)S(1)} %copy.12.counts, s32[72]{0:T(128)S(1)} %get-tuple-element.10.work, s32[1]{0:T(128)} %get-tuple-element.11.n_work, f32[260,128,128]{2,1,0:T(8,128)S(1)} %get-tuple-element.12.tiles, bf16[16,64,128]{2,1,0:T(8,128)(2,1)S(1)} %copy-done.1, ...), custom_call_target="tpu_custom_call" | custom-call | tf_op jit(solution)/shard_map/later_rows/pallas_call | solution.py:376
  237.5 0.3 collective-permute-start.5
  237.8 0.9 collective-permute-done.5.other
  238.7 74.3 %last_columns.1 = (f32[48,128]{1,0:T(8,128)S(1)}, f32[16,128]{1,0:T(8,128)}) custom-call(s32[16,16]{1,0:T(8,128)S(1)} %bitcast.11, s32[16,1]{1,0:T(8,128)S(1)} %copy.12.counts, s32[72]{0:T(128)S(1)} %get-tuple-element.10.work, s32[1]{0:T(128)} %get-tuple-element.11.n_work, f32[260,128,128]{2,1,0:T(8,128)S(1)} %get-tuple-element.12.tiles, ...), custom_call_target="tpu_custom_call" | custom-call | tf_op jit(solution)/shard_map/last_columns/pallas_call | solution.py:378
  313.1 0.0 collective-permute-start.8
  313.1 19.0 %collective-permute-start.7 = (f32[48,128]{1,0:T(8,128)S(1)}, f32[48,128]{1,0:T(8,128)S(1)}, u32[]{:S(2)}, u32[]{:S(2)}) collective-permute-start(f32[48,128]{1,0:T(8,128)S(1)} %get-tuple-element.17), channel_id=1, source_target_pairs={{0,4},{2,6},{4,0},{6,2},{8,12},{10,14},{12,8},{14,10},{1,5},{3,7},... | collective-permute-start | bytes 73736 | tf_op jit(solution)/shard_map/ppermute | solution.py:341
  332.1 1.5 collective-permute-start.6
  333.5 0.0 collective-permute-done.8
  333.5 0.7 collective-permute-done.7
  334.3 1.6 collective-permute-done.6
  335.9 1.1 collective-permute-start.9
  337.0 3.7 %collective-permute-done.9 = f32[48,128]{1,0:T(8,128)S(1)} collective-permute-done((f32[48,128]{1,0:T(8,128)S(1)}, f32[48,128]{1,0:T(8,128)S(1)}, u32[]{:S(2)}, u32[]{:S(2)}) %collective-permute-start.9) | collective-permute-done | bytes 24608 | tf_op jit(solution)/shard_map/ppermute | solution.py:341
  340.7 0.6 subtract_bitcast_fusion
  (9 shorter events, 0.1 us)
Async XLA Ops:
  1.4 1.1 copy-start
  2.5 0.9 copy-start.1
  3.4 0.7 copy-start.2
  4.1 0.7 copy-start.5
  4.9 171.4 %copy-start.3 = (f32[6144]{0:T(1024)S(1)}, f32[6144]{0:T(1024)}, u32[]{:S(2)}) copy-start(f32[6144]{0:T(1024)} %param.10) | copy-start | bytes 73732
  70.8 8.1 %collective-permute-start = (f32[16,128]{1,0:T(8,128)S(1)}, f32[16,128]{1,0:T(8,128)S(1)}, u32[]{:S(2)}, u32[]{:S(2)}) collective-permute-start(f32[16,128]{1,0:T(8,128)S(1)} %get-tuple-element.13.own), channel_id=1, source_target_pairs={{0,1},{1,0},{2,3},{3,2},{4,5},{5,4},{6,7},{7,6},{8,9},{9,8},{10,11... | collective-permute-start | bytes 24584 | tf_op jit(solution)/shard_map/ppermute | solution.py:377
  78.9 0.7 copy-start.4
  153.3 15.7 %collective-permute-start.3 = (f32[48,128]{1,0:T(8,128)S(1)}, f32[48,128]{1,0:T(8,128)S(1)}, u32[]{:S(2)}, u32[]{:S(2)}) collective-permute-start(f32[48,128]{1,0:T(8,128)S(1)} %columns.1), channel_id=1, source_target_pairs={{0,6},{2,4},{4,2},{6,0},{8,14},{10,12},{12,10},{14,8},{1,7},{3,5},... | collective-permute-start | bytes 73736 | tf_op jit(solution)/shard_map/ppermute | solution.py:341
  153.4 16.2 %collective-permute-start.2 = (f32[48,128]{1,0:T(8,128)S(1)}, f32[48,128]{1,0:T(8,128)S(1)}, u32[]{:S(2)}, u32[]{:S(2)}) collective-permute-start(f32[48,128]{1,0:T(8,128)S(1)} %columns.1), channel_id=1, source_target_pairs={{0,4},{2,6},{4,0},{6,2},{8,12},{10,14},{12,8},{14,10},{1,5},{3,7},... | collective-permute-start | bytes 73736 | tf_op jit(solution)/shard_map/ppermute | solution.py:341
  167.6 3.8 %collective-permute-start.1 = (f32[48,128]{1,0:T(8,128)S(1)}, f32[48,128]{1,0:T(8,128)S(1)}, u32[]{:S(2)}, u32[]{:S(2)}) collective-permute-start(f32[48,128]{1,0:T(8,128)S(1)} %columns.1), channel_id=1, source_target_pairs={{0,2},{2,0},{4,6},{6,4},{8,10},{10,8},{12,14},{14,12},{1,3},{3,1},... | collective-permute-start | bytes 73736 | tf_op jit(solution)/shard_map/ppermute | solution.py:341
  171.4 4.8 %collective-permute-start.4 = (f32[48,128]{1,0:T(8,128)S(1)}, f32[48,128]{1,0:T(8,128)S(1)}, u32[]{:S(2)}, u32[]{:S(2)}) collective-permute-start(f32[48,128]{1,0:T(8,128)S(1)} %multiply_add_fusion.3), channel_id=1, source_target_pairs={{0,8},{2,10},{4,12},{6,14},{8,0},{10,2},{12,4},{14,6},{1,9},{3,11}... | collective-permute-start | bytes 73736 | tf_op jit(solution)/shard_map/ppermute | solution.py:341
  237.5 1.2 collective-permute-start.5
  313.1 20.5 %collective-permute-start.8 = (f32[48,128]{1,0:T(8,128)S(1)}, f32[48,128]{1,0:T(8,128)S(1)}, u32[]{:S(2)}, u32[]{:S(2)}) collective-permute-start(f32[48,128]{1,0:T(8,128)S(1)} %get-tuple-element.17), channel_id=1, source_target_pairs={{0,6},{2,4},{4,2},{6,0},{8,14},{10,12},{12,10},{14,8},{1,7},{3,5},... | collective-permute-start | bytes 73736 | tf_op jit(solution)/shard_map/ppermute | solution.py:341
  313.1 21.2 %collective-permute-start.7 = (f32[48,128]{1,0:T(8,128)S(1)}, f32[48,128]{1,0:T(8,128)S(1)}, u32[]{:S(2)}, u32[]{:S(2)}) collective-permute-start(f32[48,128]{1,0:T(8,128)S(1)} %get-tuple-element.17), channel_id=1, source_target_pairs={{0,4},{2,6},{4,0},{6,2},{8,12},{10,14},{12,8},{14,10},{1,5},{3,7},... | collective-permute-start | bytes 73736 | tf_op jit(solution)/shard_map/ppermute | solution.py:341
  332.1 3.8 %collective-permute-start.6 = (f32[48,128]{1,0:T(8,128)S(1)}, f32[48,128]{1,0:T(8,128)S(1)}, u32[]{:S(2)}, u32[]{:S(2)}) collective-permute-start(f32[48,128]{1,0:T(8,128)S(1)} %get-tuple-element.17), channel_id=1, source_target_pairs={{0,2},{2,0},{4,6},{6,4},{8,10},{10,8},{12,14},{14,12},{1,3},{3,1},... | collective-permute-start | bytes 73736 | tf_op jit(solution)/shard_map/ppermute | solution.py:341
  335.9 4.8 %collective-permute-start.9 = (f32[48,128]{1,0:T(8,128)S(1)}, f32[48,128]{1,0:T(8,128)S(1)}, u32[]{:S(2)}, u32[]{:S(2)}) collective-permute-start(f32[48,128]{1,0:T(8,128)S(1)} %multiply_add_fusion.1), channel_id=1, source_target_pairs={{0,8},{2,10},{4,12},{6,14},{8,0},{10,2},{12,4},{14,6},{1,9},{3,11}... | collective-permute-start | bytes 73736 | tf_op jit(solution)/shard_map/ppermute | solution.py:341
